TPU v7x, 32 devices: a whole 2x2x4 slice. The times are simulated.
32 devices in a mesh: row: 8 (over z, x), col: 4 (over y, core).
Axes of the slice: x: 2, y: 2, z: 4, core: 2. Of those that a mesh axis runs over, the one named last changes fastest.
Arguments:
- mom_a: float32 [1536, 12288], P('row', 'col'), may hold values from -6 to 6
- grad_a: float32 [1536, 12288], P('row', 'col'), may hold values from -6 to 6
- basis_a: float32 [512, 12288], P('row', 'col'), may hold values from -0.0546875 to 0.0546875
- mom_b: float32 [7168, 1536], P('row', 'col'), may hold values from -6 to 6
- grad_b: float32 [7168, 1536], P('row', 'col'), may hold values from -6 to 6
- basis_b: float32 [512, 1536], P('row', 'col'), may hold values from -0.15625 to 0.15625
Outputs:
- new_mom_a: float32 [1536, 12288], P('row', 'col')
- update_a: bfloat16 [1536, 12288], P('row', 'col')
- new_basis_a: float32 [512, 12288], P('row', 'col')
- new_mom_b: float32 [7168, 1536], P('row', 'col')
- update_b: bfloat16 [7168, 1536], P('row', 'col')
- new_basis_b: float32 [512, 1536], P('row', 'col')
All inputs are finite; a program needn't handle non-finite values.
Results may differ from a plain program's by a relative error of at most 0.0049.
Values sent between devices are 32-bit elements; how exact they have to be, the bound alone decides.
A program may use at most 128 MiB of HBM per device.

v0:
```python
import math
import jax
import jax.numpy as jnp
from jax import lax
from jax.sharding import PartitionSpec as P

MU = 0.95
EPS = 1e-06


def project(buffer, basis):
    partial_proj = jnp.dot(
        buffer,
        lax.all_gather(basis, "row", axis=0, tiled=True).T,
        precision=lax.Precision.HIGHEST,
        preferred_element_type=jnp.float32,
    )
    return lax.psum(partial_proj, "col")


def local_gram(proj):
    return jnp.dot(
        proj.T, proj, precision=lax.Precision.HIGHEST, preferred_element_type=jnp.float32
    )


def single_gram(proj):
    return lax.psum(local_gram(proj), "row")


def finish(buffer, proj, gram):
    highest = lax.Precision.HIGHEST
    lower = jnp.linalg.cholesky(gram)
    ortho = lax.linalg.triangular_solve(lower, proj, left_side=False, lower=True, transpose_a=True)
    rank = ortho.shape[1]
    share_rows = rank // lax.axis_size("row")
    trans = lax.psum(
        jnp.dot(ortho.T, buffer, precision=highest, preferred_element_type=jnp.float32), "row"
    )
    squares = lax.psum(jnp.sum(trans * trans, axis=1, keepdims=True), "col")
    full_basis = trans / jnp.sqrt(squares + EPS)
    own_basis = lax.dynamic_slice_in_dim(
        full_basis, lax.axis_index("row") * share_rows, share_rows, 0
    )
    new_mom = buffer - (1.0 - MU) * jnp.dot(
        ortho, trans, precision=highest, preferred_element_type=jnp.float32
    )
    total_rows = buffer.shape[0] * lax.axis_size("row")
    total_cols = buffer.shape[1] * lax.axis_size("col")
    scale = math.sqrt(total_rows * total_cols / rank)
    update = (
        jnp.dot(ortho, full_basis, precision=highest, preferred_element_type=jnp.float32) * scale
    ).astype(jnp.bfloat16)
    return (new_mom, update, own_basis)


def shards(mom_a, grad_a, basis_a, mom_b, grad_b, basis_b):
    buffers = [MU * mom_a + grad_a, MU * mom_b + grad_b]
    projs = [project(buffers[0], basis_a), project(buffers[1], basis_b)]
    grams = [single_gram(projs[0]), single_gram(projs[1])]
    first = finish(buffers[0], projs[0], grams[0])
    second = finish(buffers[1], projs[1], grams[1])
    return (first[0], first[1], first[2], second[0], second[1], second[2])


def solution(mesh):
    return jax.shard_map(
        shards,
        mesh=mesh,
        in_specs=(
            P("row", "col"),
            P("row", "col"),
            P("row", "col"),
            P("row", "col"),
            P("row", "col"),
            P("row", "col"),
        ),
        out_specs=(
            P("row", "col"),
            P("row", "col"),
            P("row", "col"),
            P("row", "col"),
            P("row", "col"),
            P("row", "col"),
        ),
        check_vma=False,
    )
```

profile of v0, /device:TPU:0, one launch (start us, length us, event | category | flops | bytes accessed | tf_op | source)
XLA Modules:
  0.0 905.2 jit_solution(12628159477295165180)
XLA Ops:
  7.9 36.6 %all_gather.7 = f32[512,384]{1,0:T(8,128)S(1)} all-gather(f32[64,384]{1,0:T(8,128)} %param.12), channel_id=1, replica_groups=mesh['row'=8,'col'=4] {'row'}, dimensions={0}, use_global_device_ids=true | all-gather | bytes 884736 | tf_op jit(solution)/shard_map/all_gather | solution.py:14
  50.8 65.1 %all-gather.2.cloned.1.call-done = f32[512,3072]{1,0:T(8,128)} async-done(((f32[64,3072]{1,0:T(8,128)}), f32[512,3072]{1,0:T(8,128)}) %all-gather.2.cloned.1.call-update) | async-done | bytes 6291472 | tf_op jit(solution)/shard_map/all_gather | solution.py:14
  115.9 10.7 %fusion.77 = f32[192,512]{1,0:T(8,128)} fusion(f32[512,3072]{1,0:T(8,128)} %all-gather.2.cloned.1.call-done, f32[192,3072]{1,0:T(8,128)S(1)} %copy-done.1, f32[192,3072]{1,0:T(8,128)} %param.7), kind=kOutput, calls=%fused_computation.156 | convolution fusion | flops 3625058304 | bytes 11403264 | tf_op jit(solution)/shard_map/dot_general | solution.py:12
  126.6 11.9 %all-reduce.11.cloned.1.call-start = ((), (), s32[]{:S(2)}) async-start(), calls=%async_computation.2 | async-start | bytes 4194304 | tf_op jit(solution)/shard_map/psum | solution.py:28
  138.5 40.0 %all-reduce.13.cloned.1.call-done = (f32[192,512]{1,0:T(8,128)}, f32[896,512]{1,0:T(8,128)}) async-done(((f32[192,512]{1,0:T(8,128)}, f32[896,512]{1,0:T(8,128)}), (f32[192,512]{1,0:T(8,128)}, f32[896,512]{1,0:T(8,128)})) %all-reduce.13.cloned.1.call-update) | async-done | bytes 2228240 | tf_op jit(solution)/shard_map/psum | solution.py:18
  186.4 102.5 %all-reduce.11.cloned.1.call-done = (f32[512,512]{0,1:T(8,128)}, f32[512,512]{0,1:T(8,128)}) async-done(((f32[512,512]{0,1:T(8,128)}, f32[512,512]{0,1:T(8,128)}), (f32[512,512]{0,1:T(8,128)}, f32[512,512]{0,1:T(8,128)})) %all-reduce.11.cloned.1.call-update) | async-done | bytes 2097168 | tf_op jit(solution)/shard_map/psum | solution.py:28
  298.3 11.7 %cholesky.358 = f32[128,128]{1,0:T(8,128)S(1)} custom-call(f32[128,128]{1,0:T(8,128)S(1)} %cholesky.439), custom_call_target="Cholesky" | custom-call | tf_op jit(solution)/shard_map/jit(cholesky)/cholesky | solution.py:33
  310.1 9.8 %custom-call.34 = f32[1,128,128]{1,2,0:T(8,128)S(1)} custom-call(f32[1,128,128]{2,1,0:T(8,128)S(1)} %get-tuple-element.60), custom_call_target="InvertDiagBlocksLowerTriangular" | custom-call | tf_op jit(solution)/shard_map/jit(cholesky)/cholesky | solution.py:33
  323.2 11.7 %cholesky.377 = f32[128,128]{1,0:T(8,128)S(1)} custom-call(f32[128,128]{1,0:T(8,128)S(1)} %cholesky.443), custom_call_target="Cholesky" | custom-call | tf_op jit(solution)/shard_map/jit(cholesky)/cholesky | solution.py:33
  336.2 10.2 %custom-call.35 = f32[1,128,128]{1,2,0:T(8,128)S(1)} custom-call(f32[1,128,128]{2,1,0:T(8,128)S(1)} %get-tuple-element.57), custom_call_target="InvertDiagBlocksLowerTriangular" | custom-call | tf_op jit(solution)/shard_map/jit(cholesky)/cholesky | solution.py:33
  349.5 13.2 %cholesky.398 = f32[128,128]{1,0:T(8,128)} custom-call(f32[128,128]{1,0:T(8,128)} %cholesky.448), custom_call_target="Cholesky" | custom-call | tf_op jit(solution)/shard_map/jit(cholesky)/cholesky | solution.py:33
  364.9 11.3 %custom-call.36 = f32[1,128,128]{1,2,0:T(8,128)} custom-call(f32[1,128,128]{2,1,0:T(8,128)} %get-tuple-element.54), custom_call_target="InvertDiagBlocksLowerTriangular" | custom-call | tf_op jit(solution)/shard_map/jit(cholesky)/cholesky | solution.py:33
  378.5 11.9 %cholesky.415 = f32[128,128]{1,0:T(8,128)S(1)} custom-call(f32[128,128]{1,0:T(8,128)S(1)} %convolution_subtract_fusion.9), custom_call_target="Cholesky" | custom-call | tf_op jit(solution)/shard_map/jit(cholesky)/cholesky | solution.py:33
  394.7 11.6 %while.3 = (s32[]{:T(128)}, f32[512,512]{1,0:T(8,128)}, s32[4,2]{0,1:T(2,128)S(1)}, f32[4,128,128]{2,1,0:T(8,128)S(1)}, s32[]{:T(128)}) while((s32[]{:T(128)}, f32[512,512]{1,0:T(8,128)}, s32[4,2]{0,1:T(2,128)S(1)}, f32[4,128,128]{2,1,0:T(8,128)S(1)}, s32[]{:T(128)}) %tuple.56), condition=%wide.while_cond.1, body=%wide.while_body.1.sunk | while | flops 2 | bytes 131181 | solution.py:34
  406.3 39.3 %custom-call.27 = f32[4,128,128]{1,2,0:T(8,128)S(1)} custom-call(f32[4,128,128]{2,1,0:T(8,128)S(1)} %get-tuple-element.22), custom_call_target="InvertDiagBlocksLowerTriangular" | custom-call | tf_op jit(solution)/shard_map/triangular_solve | solution.py:34
  462.4 12.1 %cholesky.286 = f32[128,128]{1,0:T(8,128)S(1)} custom-call(f32[128,128]{1,0:T(8,128)S(1)} %cholesky.426), custom_call_target="Cholesky" | custom-call | tf_op jit(solution)/shard_map/jit(cholesky)/cholesky | solution.py:33
  474.5 9.8 %custom-call.31 = f32[1,128,128]{1,2,0:T(8,128)S(1)} custom-call(f32[1,128,128]{2,1,0:T(8,128)S(1)} %get-tuple-element.70), custom_call_target="InvertDiagBlocksLowerTriangular" | custom-call | tf_op jit(solution)/shard_map/jit(cholesky)/cholesky | solution.py:33
  488.6 12.3 %cholesky.305 = f32[128,128]{1,0:T(8,128)} custom-call(f32[128,128]{1,0:T(8,128)S(1)} %cholesky.430), custom_call_target="Cholesky" | custom-call | tf_op jit(solution)/shard_map/jit(cholesky)/cholesky | solution.py:33
  503.8 10.4 %custom-call.32 = f32[1,128,128]{1,2,0:T(8,128)} custom-call(f32[1,128,128]{2,1,0:T(8,128)S(1)} %get-tuple-element.67), custom_call_target="InvertDiagBlocksLowerTriangular" | custom-call | tf_op jit(solution)/shard_map/jit(cholesky)/cholesky | solution.py:33
  517.5 11.9 %cholesky.326 = f32[128,128]{1,0:T(8,128)S(1)} custom-call(f32[128,128]{1,0:T(8,128)S(1)} %cholesky.435), custom_call_target="Cholesky" | custom-call | tf_op jit(solution)/shard_map/jit(cholesky)/cholesky | solution.py:33
  542.7 11.7 %cholesky.343 = f32[128,128]{1,0:T(8,128)S(1)} custom-call(f32[128,128]{1,0:T(8,128)S(1)} %convolution_subtract_fusion.10), custom_call_target="Cholesky" | custom-call | tf_op jit(solution)/shard_map/jit(cholesky)/cholesky | solution.py:33
  560.7 11.6 %while.2 = (s32[]{:T(128)}, f32[512,512]{1,0:T(8,128)}, s32[4,2]{0,1:T(2,128)S(1)}, f32[4,128,128]{2,1,0:T(8,128)S(1)}, s32[]{:T(128)}) while((s32[]{:T(128)}, f32[512,512]{1,0:T(8,128)}, s32[4,2]{0,1:T(2,128)S(1)}, f32[4,128,128]{2,1,0:T(8,128)S(1)}, s32[]{:T(128)}) %tuple.70), condition=%wide.while_cond, body=%wide.while_body.sunk | while | flops 2 | bytes 131181 | solution.py:34
  572.2 40.2 %custom-call.26 = f32[4,128,128]{1,2,0:T(8,128)} custom-call(f32[4,128,128]{2,1,0:T(8,128)S(1)} %get-tuple-element.14), custom_call_target="InvertDiagBlocksLowerTriangular" | custom-call | tf_op jit(solution)/shard_map/triangular_solve | solution.py:34
  628.7 231.0 %all-reduce.9.cloned.1.call-done = (f32[512,3072]{1,0:T(8,128)}, f32[512,384]{1,0:T(8,128)}) async-done(((f32[512,3072]{1,0:T(8,128)}, f32[512,384]{1,0:T(8,128)}), (f32[512,3072]{1,0:T(8,128)}, f32[512,384]{1,0:T(8,128)})) %all-reduce.9.cloned.1.call-update) | async-done | bytes 7077904 | tf_op jit(solution)/shard_map/psum | solution.py:37
  (148 shorter events, 159.9 us)
Async XLA Ops:
  7.2 108.7 %all-gather.2.cloned.1.call-start = ((), (), s32[]{:S(2)}) async-start(), calls=%async_computation | async-start | bytes 7077888 | tf_op jit(solution)/shard_map/all_gather | solution.py:14
  7.9 170.6 %all-reduce.13.cloned.1.call-start = ((), (), s32[]{:S(2)}) async-start(), calls=%async_computation.3 | async-start | bytes 4456448 | tf_op jit(solution)/shard_map/psum | solution.py:18
  44.6 71.3 %copy-start.1 = (f32[192,3072]{1,0:T(8,128)S(1)}, f32[192,3072]{1,0:T(8,128)}, u32[]{:S(2)}) copy-start(f32[192,3072]{1,0:T(8,128)} %param.8) | copy-start | bytes 7077892
  126.6 162.3 %all-reduce.11.cloned.1.call-start = ((), (), s32[]{:S(2)}) async-start(), calls=%async_computation.2 | async-start | bytes 4194304 | tf_op jit(solution)/shard_map/psum | solution.py:28
  178.5 3.3 copy-start.4
  186.4 673.4 %all-reduce.9.cloned.1.call-start = ((), (), s32[]{:S(2)}) async-start(), calls=%async_computation.1 | async-start | bytes 14155776 | tf_op jit(solution)/shard_map/psum | solution.py:37
  288.9 5.2 copy-start.9
  297.4 1.0 copy-start.11
  322.5 0.7 copy-start.16
  445.6 4.4 copy-start.5
  453.1 8.4 copy-start.8
  453.1 4.2 copy-start.6
  453.1 4.2 copy-start.7
  457.3 4.2 copy-start.10
  612.4 9.2 %copy-start.2 = (f32[192,3072]{1,0:T(8,128)S(1)}, f32[192,3072]{1,0:T(8,128)}, u32[]{:S(2)}) copy-start(f32[192,3072]{1,0:T(8,128)} %param.7) | copy-start | bytes 7077892
  618.3 2.6 copy-start.12
  620.9 0.6 copy-start.14
  861.0 6.6 copy-start
  876.0 16.1 %slice-start = ((s8[6291456]{0:T(1024)(128)(4,1)}), s8[4194304]{0:T(1024)(128)(4,1)S(1)}, s32[]{:S(2)}) async-start(s8[6291456]{0:T(1024)(128)(4,1)} %bitcast.110), calls=%async_computation.4 | async-start | bytes 8388608
  881.9 3.8 copy-start.13
  881.9 3.8 copy-start.15
  881.9 10.2 %slice-start.1 = ((s8[6291456]{0:T(1024)(128)(4,1)}), s8[2097152]{0:T(1024)(128)(4,1)S(1)}, s32[]{:S(2)}) async-start(s8[6291456]{0:T(1024)(128)(4,1)} %bitcast.110), calls=%async_computation.5 | async-start | bytes 4194304
  885.7 6.4 copy-start.3
Sparse Core Ops, SparseCore 0:
  10.2 105.6 all-gather.1
  126.7 51.7 all-reduce.12
  186.5 102.3 all-reduce.10
  628.8 230.8 all-reduce.8
where the time goes:
time: 913 us; the launch traced here: 905 us
  waiting for transfers between devices  439 us (48%)
  other arithmetic  261 us (29%)
  matrix products  95.3 us (10%)
  blocking collectives  43.2 us (5%)
  local copies, waits for them, and re-layouts  34.8 us (4%)
  between operations  19.9 us (2%)
  starting transfers between devices  12 us (1%)
    psum x1, waiting for transfers between devices, finish(): lax.psum(jnp.dot(ortho.T, buffer, precision=highest, preferred_element_ty...  231 us
    another operation x30, other arithmetic, finish(): lower = jnp.linalg.cholesky(gram)  167 us
    psum x1, waiting for transfers between devices, single_gram(): return lax.psum(local_gram(proj), 'row')  102 us
    another operation x5, other arithmetic, finish(): lax.linalg.triangular_solve(lower, proj, left_side=False, lower=True, tra...  82.9 us
    all_gather x1, waiting for transfers between devices, project(): lax.all_gather(basis, 'row', axis=0, tiled=True)  65.1 us
    psum x1, waiting for transfers between devices, project(): return lax.psum(partial_proj, 'col')  40 us
    all_gather x1, blocking collectives, project(): lax.all_gather(basis, 'row', axis=0, tiled=True)  36.6 us
    another operation x24, local copies, waits for them, and re-layouts  23 us
  transfers between devices with their start and end apart: 4, of which 4 were waited for; matrix products, arithmetic and copies ran while one was open for 1% of the time, Pallas kernels for 0%

commit v1 on v0

--- a/solution.py
+++ b/solution.py
@@ -34,8 +34,12 @@
     ortho = lax.linalg.triangular_solve(lower, proj, left_side=False, lower=True, transpose_a=True)
     rank = ortho.shape[1]
     share_rows = rank // lax.axis_size("row")
-    trans = lax.psum(
-        jnp.dot(ortho.T, buffer, precision=highest, preferred_element_type=jnp.float32), "row"
+    trans = jnp.sum(
+        lax.all_gather(
+            jnp.dot(ortho.T, buffer, precision=highest, preferred_element_type=jnp.float32),
+            axis_name="row",
+        ),
+        0,
     )
     squares = lax.psum(jnp.sum(trans * trans, axis=1, keepdims=True), "col")
     full_basis = trans / jnp.sqrt(squares + EPS)

time: 913 us -> 1650 us (1.81)
  waiting for transfers between devices: 439 us -> 1150 us
  other arithmetic: 261 us -> 285 us
    all_gather x0 -> x2, waiting for transfers between devices: none -> 939 us  [finish(): lax.all_gather(jnp.dot(ortho.T, buffer, precision=highest, preferred_elem...]
    psum x1 -> x0, waiting for transfers between devices: 231 us -> none  [finish(): lax.psum(jnp.dot(ortho.T, buffer, precision=highest, preferred_element_ty...]
    reduce_sum x0 -> x2, other arithmetic: none -> 25.3 us  [finish(): jnp.sum(lax.all_gather(jnp.dot(ortho.T, buffer, precision=highest, prefer...]
  transfers between devices with their start and end apart: 4 -> 5, of which waited for: 4 -> 4; matrix products, arithmetic and copies ran while one was open for 1% -> 11% of each run, Pallas kernels for 0% -> 0%
where the time goes in v1:
time: 1650 us; the launch traced here: 1640 us
  waiting for transfers between devices  1150 us (70%)
  other arithmetic  285 us (17%)
  matrix products  94.9 us (6%)
  blocking collectives  43.2 us (3%)
  local copies, waits for them, and re-layouts  36.2 us (2%)
  between operations  19.6 us (1%)
    all_gather x2, waiting for transfers between devices, finish(): lax.all_gather(jnp.dot(ortho.T, buffer, precision=highest, preferred_elem...  939 us
    another operation x30, other arithmetic, finish(): lower = jnp.linalg.cholesky(gram)  167 us
    psum x1, waiting for transfers between devices, single_gram(): return lax.psum(local_gram(proj), 'row')  102 us
    another operation x5, other arithmetic, finish(): lax.linalg.triangular_solve(lower, proj, left_side=False, lower=True, tra...  82.7 us
    all_gather x1, waiting for transfers between devices, project(): lax.all_gather(basis, 'row', axis=0, tiled=True)  65.1 us
    psum x1, waiting for transfers between devices, project(): return lax.psum(partial_proj, 'col')  40 us
    all_gather x1, blocking collectives, project(): lax.all_gather(basis, 'row', axis=0, tiled=True)  36.6 us
  transfers between devices with their start and end apart: 5, of which 4 were waited for; matrix products, arithmetic and copies ran while one was open for 11% of the time, Pallas kernels for 0%

profile of v1, /device:TPU:0, one launch (start us, length us, event | category | flops | bytes accessed | tf_op | source)
XLA Modules:
  0.0 1639.5 jit_solution(7140545406466221056)
XLA Ops:
  7.9 36.6 %all_gather.21 = f32[512,384]{1,0:T(8,128)S(1)} all-gather(f32[64,384]{1,0:T(8,128)} %param.12), channel_id=1, replica_groups=mesh['row'=8,'col'=4] {'row'}, dimensions={0}, use_global_device_ids=true | all-gather | bytes 884736 | tf_op jit(solution)/shard_map/all_gather | solution.py:14
  50.8 65.1 %all-gather.6.cloned.1.call-done = f32[512,3072]{1,0:T(8,128)} async-done(((f32[64,3072]{1,0:T(8,128)}), f32[512,3072]{1,0:T(8,128)}) %all-gather.6.cloned.1.call-update) | async-done | bytes 6291472 | tf_op jit(solution)/shard_map/all_gather | solution.py:14
  115.9 10.7 fusion.77
  126.6 11.9 all-reduce.7.cloned.1.call-start
  138.5 40.0 %all-reduce.9.cloned.1.call-done = (f32[192,512]{1,0:T(8,128)}, f32[896,512]{1,0:T(8,128)}) async-done(((f32[192,512]{1,0:T(8,128)}, f32[896,512]{1,0:T(8,128)}), (f32[192,512]{1,0:T(8,128)}, f32[896,512]{1,0:T(8,128)})) %all-reduce.9.cloned.1.call-update) | async-done | bytes 2228240 | tf_op jit(solution)/shard_map/psum | solution.py:18
  186.4 102.5 %all-reduce.7.cloned.1.call-done = (f32[512,512]{0,1:T(8,128)}, f32[512,512]{0,1:T(8,128)}) async-done(((f32[512,512]{0,1:T(8,128)}, f32[512,512]{0,1:T(8,128)}), (f32[512,512]{0,1:T(8,128)}, f32[512,512]{0,1:T(8,128)})) %all-reduce.7.cloned.1.call-update) | async-done | bytes 2097168 | tf_op jit(solution)/shard_map/psum | solution.py:28
  298.3 11.7 cholesky.358
  323.2 11.7 cholesky.377
  336.2 10.2 custom-call.35
  349.5 13.2 cholesky.398
  364.9 11.3 custom-call.36
  378.5 11.9 cholesky.415
  394.7 11.6 while.3
  406.3 39.3 %custom-call.27 = f32[4,128,128]{1,2,0:T(8,128)S(1)} custom-call(f32[4,128,128]{2,1,0:T(8,128)S(1)} %get-tuple-element.22), custom_call_target="InvertDiagBlocksLowerTriangular" | custom-call | tf_op jit(solution)/shard_map/triangular_solve | solution.py:34
  463.6 11.7 cholesky.286
  475.4 9.8 custom-call.31
  490.1 12.5 cholesky.305
  503.3 10.8 custom-call.32
  516.5 11.7 cholesky.326
  540.9 11.7 cholesky.343
  560.7 12.0 while.2
  572.7 39.9 %custom-call.26 = f32[4,128,128]{1,2,0:T(8,128)} custom-call(f32[4,128,128]{2,1,0:T(8,128)S(1)} %get-tuple-element.14), custom_call_target="InvertDiagBlocksLowerTriangular" | custom-call | tf_op jit(solution)/shard_map/triangular_solve | solution.py:34
  641.2 939.5 %all-gather.8.cloned.1.call-done = f32[4096,3072]{1,0:T(8,128)} async-done(((f32[512,3072]{1,0:T(8,128)}), f32[4096,3072]{1,0:T(8,128)}) %all-gather.8.cloned.1.call-update) | async-done | bytes 50331664 | tf_op jit(solution)/shard_map/all_gather | solution.py:38
  1580.7 21.2 %reduce_sum.36 = f32[512,3072]{1,0:T(8,128)} reduce(f32[8,512,3072]{2,1,0:T(8,128)} %bitcast.112, f32[]{:T(128)} %constant.124.clone.1), dimensions={0}, to_apply=%region_10.12 | reduce | flops 11010048 | bytes 56623108 | tf_op jit(solution)/shard_map/reduce_sum | solution.py:37
  (148 shorter events, 174.5 us)
Async XLA Ops:
  7.2 108.7 %all-gather.6.cloned.1.call-start = ((), (), s32[]{:S(2)}) async-start(), calls=%async_computation | async-start | bytes 7077888 | tf_op jit(solution)/shard_map/all_gather | solution.py:14
  7.9 170.6 %all-reduce.9.cloned.1.call-start = ((), (), s32[]{:S(2)}) async-start(), calls=%async_computation.4 | async-start | bytes 4456448 | tf_op jit(solution)/shard_map/psum | solution.py:18
  44.6 71.3 %copy-start.1 = (f32[192,3072]{1,0:T(8,128)S(1)}, f32[192,3072]{1,0:T(8,128)}, u32[]{:S(2)}) copy-start(f32[192,3072]{1,0:T(8,128)} %param.8) | copy-start | bytes 7077892
  126.6 162.3 %all-reduce.7.cloned.1.call-start = ((), (), s32[]{:S(2)}) async-start(), calls=%async_computation.3 | async-start | bytes 4194304 | tf_op jit(solution)/shard_map/psum | solution.py:28
  178.5 3.3 copy-start.4
  186.4 442.7 %all-gather.10.cloned.1.call-start = ((), (), s32[]{:S(2)}) async-start(), calls=%async_computation.2 | async-start | bytes 7077888 | tf_op jit(solution)/shard_map/all_gather | solution.py:38
  288.9 5.2 copy-start.9
  297.4 1.0 copy-start.11
  322.5 0.7 copy-start.16
  445.6 4.4 copy-start.5
  453.1 4.2 copy-start.8
  453.1 4.9 copy-start.6
  453.1 4.9 copy-start.7
  457.3 0.8 copy-start.10
  462.3 1118.4 %all-gather.8.cloned.1.call-start = ((), (), s32[]{:S(2)}) async-start(), calls=%async_computation.1 | async-start | bytes 56623104 | tf_op jit(solution)/shard_map/all_gather | solution.py:38
  612.7 9.2 copy-start.2
  618.6 2.6 copy-start.12
  621.2 0.6 copy-start.14
  1611.8 7.5 copy-start
  1619.3 1.0 copy-start.13
  1619.3 1.0 copy-start.15
  1620.3 6.4 copy-start.3
Sparse Core Ops, SparseCore 0:
  10.2 105.6 all-gather.5
  126.7 51.7 all-reduce.8
  186.5 102.3 all-reduce.6
  462.4 98.1 all-gather.9
  629.1 951.5 all-gather.7
